TPU v7x, 128 devices: a whole 4x4x4 slice. The times are simulated.
128 devices in a mesh: row: 16 (over y_lo, x, core), col: 8 (over y_hi, z).
Axes of the slice: x: 4, y: 4 (y_hi: 2, y_lo: 2; y = y_hi * 2 + y_lo), z: 4, core: 2. Of those that a mesh axis runs over, the one named last changes fastest.
Arguments:
- density: bfloat16 [6144, 6144], P(('row', 'col')), may hold values from -0.49023438 to 0.49023438
- pattern: int32 [48, 48], replicated, may hold values 0 or 1
- filter_square: int32 [48, 48], replicated, may hold values 0 or 1
- filter_cube: int32 [48, 48], replicated, may hold values 0 or 1
Outputs:
- purified: float32 [6144, 6144], P('row', 'col')
All inputs are finite; a program needn't handle non-finite values.
Results may differ from a plain program's by a relative error of at most 0.0027.
Values may be sent and summed in bfloat16 or wider, within the bound.
A program may use at most 64 MiB of HBM per device.

v0:
```python
import jax
import jax.numpy as jnp
from jax import lax
from jax.sharding import PartitionSpec as P

BLK = 128


def shifted(block, axis, distance):
    devices = range(lax.axis_size(axis))
    route = [((i - distance) % len(devices), i) for i in devices]
    return lax.ppermute(block, axis, route)


def tile_mask(mask, row_id, col_id, piece_rows, width):
    row_blocks = piece_rows // BLK
    col_blocks = width // BLK
    small = lax.dynamic_slice(
        mask, (row_id * row_blocks, col_id * col_blocks), (row_blocks, col_blocks)
    ).astype(jnp.float32)
    return jnp.broadcast_to(small[:, None, :, None], (row_blocks, BLK, col_blocks, BLK)).reshape(
        piece_rows, width
    )


def skew(tile_now, col_id, col_count, stride):
    for bit_number in range(col_count.bit_length() - 1):
        moved = shifted(tile_now, "row", -(stride << bit_number))
        tile_now = jnp.where(col_id >> bit_number & 1 == 1, moved, tile_now)
    return tile_now


def move_right(right_now):
    return shifted(right_now, "row", -1)


def cannon(right_tile, fetch, advance, state, groups, inner):
    total = jnp.zeros((right_tile.shape[0], right_tile.shape[1]), jnp.float32)

    def one_group(group, carry):
        total, right_now, state = carry
        total = total + jnp.dot(
            fetch(state, group * inner + 0, 0), right_now, preferred_element_type=jnp.float32
        )
        right_now = move_right(right_now)
        state = advance(state, group)
        return (total, right_now, state)

    total, right_now, state = lax.fori_loop(0, groups - 1, one_group, (total, right_tile, state))
    total = total + jnp.dot(
        fetch(state, (groups - 1) * inner, 0), right_now, preferred_element_type=jnp.float32
    )
    return (total, state)


def on_device(density, pattern, filter_square, filter_cube):
    row_count = lax.axis_size("row")
    col_count = lax.axis_size("col")
    row_id = lax.axis_index("row")
    col_id = lax.axis_index("col")
    rows_one, order = density.shape
    nblocks = pattern.shape[0]
    piece_cols = order // row_count
    width = order // col_count
    factor = row_count // col_count
    first = (row_id * col_count + col_id) * rows_one
    block_of = (first + jnp.arange(rows_one, dtype=jnp.int32)) // BLK
    onehot = (block_of[:, None] == jnp.arange(nblocks, dtype=jnp.int32)[None, :]).astype(
        jnp.float32
    )
    row_mask = jnp.dot(onehot, pattern.astype(jnp.float32))
    full_mask = jnp.broadcast_to(row_mask[:, :, None], (rows_one, nblocks, BLK)).reshape(
        rows_one, order
    )
    local = density * full_mask.astype(jnp.bfloat16)
    grid_source = local.reshape(rows_one, 1, col_count, width)

    def fetch_slot(state, step, slot):
        return state[:, 0, :]

    def wrap_fix(moved):
        return jnp.where(col_id == col_count - 1, jnp.roll(moved, -1, axis=1), moved)

    def advance_shift(state, step):
        return wrap_fix(shifted(state, "col", -1))

    rolled = jnp.roll(local.reshape(rows_one, row_count, piece_cols), -row_id, axis=1)
    aligned_source = rolled.reshape(rows_one, factor, col_count, piece_cols)
    grid_tile, aligned = (
        lax.all_to_all(grid_source, "col", split_axis=2, concat_axis=0, tiled=True),
        lax.all_to_all(aligned_source, "col", split_axis=2, concat_axis=0, tiled=True),
    )
    grid_tile = grid_tile.reshape(piece_cols, width)
    aligned = aligned.reshape(piece_cols, factor, piece_cols)
    right_first = skew(grid_tile, col_id, col_count, 1)
    square_sum, unused = cannon(right_first, fetch_slot, advance_shift, aligned, row_count, 1)
    square = square_sum * tile_mask(filter_square, row_id, col_id, piece_cols, width)
    square_half = square.astype(jnp.bfloat16)
    right_second = skew(square_half, col_id, col_count, 1)
    cube_sum, unused = cannon(right_second, fetch_slot, advance_shift, aligned, row_count, 1)
    cube = cube_sum * tile_mask(filter_cube, row_id, col_id, piece_cols, width)
    return 3.0 * square - 2.0 * cube


def solution(mesh):
    placed = (P(("row", "col"), None), P(), P(), P())
    return jax.shard_map(
        on_device, mesh=mesh, in_specs=placed, out_specs=P("row", "col"), check_vma=False
    )
```

profile of v0, /device:TPU:126, one launch (start us, length us, event | category | flops | bytes accessed | tf_op | source)
XLA Modules:
  0.0 880.0 jit_solution(17764537809108270512)
XLA Ops:
  71.4 393.5 %while.34 = (s32[]{:T(128)}, f32[384,768]{1,0:T(8,128)S(1)}, bf16[384,768]{1,0:T(8,128)(2,1)S(1)}, bf16[384,2,384]{2,0,1:T(8,128)(2,1)}, pred[]{:T(512)}, /*index=5*/s32[]{:T(128)}, s32[]{:T(128)}) while((s32[]{:T(128)}, f32[384,768]{1,0:T(8,128)S(1)}, bf16[384,768]{1,0:T(8,128)(2,1)S(1)}, bf16[384,2,384]{2,0,1:T(8,128)(2,1)}, ...), condition=%wide.region_1.2_spmd.clone, body=%wide.region_0.1_spmd.clone.sunk | while | flops 227672064 | bytes 12091560 | solution.py:49
  74.1 22.9 %collective-permute-done.1 = bf16[384,2,384]{2,0,1:T(8,128)(2,1)S(1)} collective-permute-done((bf16[384,2,384]{2,0,1:T(8,128)(2,1)}, bf16[384,2,384]{2,0,1:T(8,128)(2,1)S(1)}, u32[]{:S(2)}, u32[]{:S(2)}) %collective-permute-start.1) | collective-permute-done | bytes 589856 | tf_op jit(solution)/shard_map/while/body/eval_jaxpr/ppermute | solution.py:12
  99.8 22.8 %collective-permute-done.1 = bf16[384,2,384]{2,0,1:T(8,128)(2,1)S(1)} collective-permute-done((bf16[384,2,384]{2,0,1:T(8,128)(2,1)}, bf16[384,2,384]{2,0,1:T(8,128)(2,1)S(1)}, u32[]{:S(2)}, u32[]{:S(2)}) %collective-permute-start.1) | collective-permute-done | bytes 589856 | tf_op jit(solution)/shard_map/while/body/eval_jaxpr/ppermute | solution.py:12
  221.0 25.7 %collective-permute-done.1 = bf16[384,2,384]{2,0,1:T(8,128)(2,1)S(1)} collective-permute-done((bf16[384,2,384]{2,0,1:T(8,128)(2,1)}, bf16[384,2,384]{2,0,1:T(8,128)(2,1)S(1)}, u32[]{:S(2)}, u32[]{:S(2)}) %collective-permute-start.1) | collective-permute-done | bytes 589856 | tf_op jit(solution)/shard_map/while/body/eval_jaxpr/ppermute | solution.py:12
  249.5 23.5 %collective-permute-done.1 = bf16[384,2,384]{2,0,1:T(8,128)(2,1)S(1)} collective-permute-done((bf16[384,2,384]{2,0,1:T(8,128)(2,1)}, bf16[384,2,384]{2,0,1:T(8,128)(2,1)S(1)}, u32[]{:S(2)}, u32[]{:S(2)}) %collective-permute-start.1) | collective-permute-done | bytes 589856 | tf_op jit(solution)/shard_map/while/body/eval_jaxpr/ppermute | solution.py:12
  300.5 27.9 %collective-permute-done.1 = bf16[384,2,384]{2,0,1:T(8,128)(2,1)S(1)} collective-permute-done((bf16[384,2,384]{2,0,1:T(8,128)(2,1)}, bf16[384,2,384]{2,0,1:T(8,128)(2,1)S(1)}, u32[]{:S(2)}, u32[]{:S(2)}) %collective-permute-start.1) | collective-permute-done | bytes 589856 | tf_op jit(solution)/shard_map/while/body/eval_jaxpr/ppermute | solution.py:12
  331.2 23.6 %collective-permute-done.1 = bf16[384,2,384]{2,0,1:T(8,128)(2,1)S(1)} collective-permute-done((bf16[384,2,384]{2,0,1:T(8,128)(2,1)}, bf16[384,2,384]{2,0,1:T(8,128)(2,1)S(1)}, u32[]{:S(2)}, u32[]{:S(2)}) %collective-permute-start.1) | collective-permute-done | bytes 589856 | tf_op jit(solution)/shard_map/while/body/eval_jaxpr/ppermute | solution.py:12
  357.6 22.7 %collective-permute-done.1 = bf16[384,2,384]{2,0,1:T(8,128)(2,1)S(1)} collective-permute-done((bf16[384,2,384]{2,0,1:T(8,128)(2,1)}, bf16[384,2,384]{2,0,1:T(8,128)(2,1)S(1)}, u32[]{:S(2)}, u32[]{:S(2)}) %collective-permute-start.1) | collective-permute-done | bytes 589856 | tf_op jit(solution)/shard_map/while/body/eval_jaxpr/ppermute | solution.py:12
  383.1 22.6 %collective-permute-done.1 = bf16[384,2,384]{2,0,1:T(8,128)(2,1)S(1)} collective-permute-done((bf16[384,2,384]{2,0,1:T(8,128)(2,1)}, bf16[384,2,384]{2,0,1:T(8,128)(2,1)S(1)}, u32[]{:S(2)}, u32[]{:S(2)}) %collective-permute-start.1) | collective-permute-done | bytes 589856 | tf_op jit(solution)/shard_map/while/body/eval_jaxpr/ppermute | solution.py:12
  408.6 36.2 %collective-permute-done.1 = bf16[384,2,384]{2,0,1:T(8,128)(2,1)S(1)} collective-permute-done((bf16[384,2,384]{2,0,1:T(8,128)(2,1)}, bf16[384,2,384]{2,0,1:T(8,128)(2,1)S(1)}, u32[]{:S(2)}, u32[]{:S(2)}) %collective-permute-start.1) | collective-permute-done | bytes 589856 | tf_op jit(solution)/shard_map/while/body/eval_jaxpr/ppermute | solution.py:12
  511.2 365.5 %while.35 = (s32[]{:T(128)}, f32[384,768]{1,0:T(8,128)S(1)}, bf16[384,768]{1,0:T(8,128)(2,1)S(1)}, bf16[384,2,384]{2,0,1:T(8,128)(2,1)S(1)}, pred[]{:T(512)}, /*index=5*/s32[]{:T(128)}, s32[]{:T(128)}) while((s32[]{:T(128)}, f32[384,768]{1,0:T(8,128)S(1)}, bf16[384,768]{1,0:T(8,128)(2,1)S(1)}, bf16[384,2,384]{2,0,1:T(8,128)(2,1)S(1)}, ...), condition=%wide.region_3.4_spmd.clone, body=%wide.region_2.3_spmd.clone.sunk | while | flops 227672064 | bytes 12091560 | solution.py:49
  533.3 24.4 %collective-permute-done.3 = bf16[384,2,384]{2,0,1:T(8,128)(2,1)S(1)} collective-permute-done((bf16[384,2,384]{2,0,1:T(8,128)(2,1)S(1)}, bf16[384,2,384]{2,0,1:T(8,128)(2,1)S(1)}, u32[]{:S(2)}, u32[]{:S(2)}) %collective-permute-start.3) | collective-permute-done | bytes 589856 | tf_op jit(solution)/shard_map/while/body/eval_jaxpr/ppermute | solution.py:12
  558.7 23.9 %collective-permute-done.3 = bf16[384,2,384]{2,0,1:T(8,128)(2,1)S(1)} collective-permute-done((bf16[384,2,384]{2,0,1:T(8,128)(2,1)S(1)}, bf16[384,2,384]{2,0,1:T(8,128)(2,1)S(1)}, u32[]{:S(2)}, u32[]{:S(2)}) %collective-permute-start.3) | collective-permute-done | bytes 589856 | tf_op jit(solution)/shard_map/while/body/eval_jaxpr/ppermute | solution.py:12
  583.7 22.7 %collective-permute-done.3 = bf16[384,2,384]{2,0,1:T(8,128)(2,1)S(1)} collective-permute-done((bf16[384,2,384]{2,0,1:T(8,128)(2,1)S(1)}, bf16[384,2,384]{2,0,1:T(8,128)(2,1)S(1)}, u32[]{:S(2)}, u32[]{:S(2)}) %collective-permute-start.3) | collective-permute-done | bytes 589856 | tf_op jit(solution)/shard_map/while/body/eval_jaxpr/ppermute | solution.py:12
  607.5 28.1 %collective-permute-done.3 = bf16[384,2,384]{2,0,1:T(8,128)(2,1)S(1)} collective-permute-done((bf16[384,2,384]{2,0,1:T(8,128)(2,1)S(1)}, bf16[384,2,384]{2,0,1:T(8,128)(2,1)S(1)}, u32[]{:S(2)}, u32[]{:S(2)}) %collective-permute-start.3) | collective-permute-done | bytes 589856 | tf_op jit(solution)/shard_map/while/body/eval_jaxpr/ppermute | solution.py:12
  636.7 24.2 %collective-permute-done.3 = bf16[384,2,384]{2,0,1:T(8,128)(2,1)S(1)} collective-permute-done((bf16[384,2,384]{2,0,1:T(8,128)(2,1)S(1)}, bf16[384,2,384]{2,0,1:T(8,128)(2,1)S(1)}, u32[]{:S(2)}, u32[]{:S(2)}) %collective-permute-start.3) | collective-permute-done | bytes 589856 | tf_op jit(solution)/shard_map/while/body/eval_jaxpr/ppermute | solution.py:12
  661.9 22.1 %collective-permute-done.3 = bf16[384,2,384]{2,0,1:T(8,128)(2,1)S(1)} collective-permute-done((bf16[384,2,384]{2,0,1:T(8,128)(2,1)S(1)}, bf16[384,2,384]{2,0,1:T(8,128)(2,1)S(1)}, u32[]{:S(2)}, u32[]{:S(2)}) %collective-permute-start.3) | collective-permute-done | bytes 589856 | tf_op jit(solution)/shard_map/while/body/eval_jaxpr/ppermute | solution.py:12
  685.1 23.7 %collective-permute-done.3 = bf16[384,2,384]{2,0,1:T(8,128)(2,1)S(1)} collective-permute-done((bf16[384,2,384]{2,0,1:T(8,128)(2,1)S(1)}, bf16[384,2,384]{2,0,1:T(8,128)(2,1)S(1)}, u32[]{:S(2)}, u32[]{:S(2)}) %collective-permute-start.3) | collective-permute-done | bytes 589856 | tf_op jit(solution)/shard_map/while/body/eval_jaxpr/ppermute | solution.py:12
  709.9 23.7 %collective-permute-done.3 = bf16[384,2,384]{2,0,1:T(8,128)(2,1)S(1)} collective-permute-done((bf16[384,2,384]{2,0,1:T(8,128)(2,1)S(1)}, bf16[384,2,384]{2,0,1:T(8,128)(2,1)S(1)}, u32[]{:S(2)}, u32[]{:S(2)}) %collective-permute-start.3) | collective-permute-done | bytes 589856 | tf_op jit(solution)/shard_map/while/body/eval_jaxpr/ppermute | solution.py:12
  734.6 23.7 %collective-permute-done.3 = bf16[384,2,384]{2,0,1:T(8,128)(2,1)S(1)} collective-permute-done((bf16[384,2,384]{2,0,1:T(8,128)(2,1)S(1)}, bf16[384,2,384]{2,0,1:T(8,128)(2,1)S(1)}, u32[]{:S(2)}, u32[]{:S(2)}) %collective-permute-start.3) | collective-permute-done | bytes 589856 | tf_op jit(solution)/shard_map/while/body/eval_jaxpr/ppermute | solution.py:12
  759.4 23.7 %collective-permute-done.3 = bf16[384,2,384]{2,0,1:T(8,128)(2,1)S(1)} collective-permute-done((bf16[384,2,384]{2,0,1:T(8,128)(2,1)S(1)}, bf16[384,2,384]{2,0,1:T(8,128)(2,1)S(1)}, u32[]{:S(2)}, u32[]{:S(2)}) %collective-permute-start.3) | collective-permute-done | bytes 589856 | tf_op jit(solution)/shard_map/while/body/eval_jaxpr/ppermute | solution.py:12
  784.1 23.7 %collective-permute-done.3 = bf16[384,2,384]{2,0,1:T(8,128)(2,1)S(1)} collective-permute-done((bf16[384,2,384]{2,0,1:T(8,128)(2,1)S(1)}, bf16[384,2,384]{2,0,1:T(8,128)(2,1)S(1)}, u32[]{:S(2)}, u32[]{:S(2)}) %collective-permute-start.3) | collective-permute-done | bytes 589856 | tf_op jit(solution)/shard_map/while/body/eval_jaxpr/ppermute | solution.py:12
  808.9 23.7 %collective-permute-done.3 = bf16[384,2,384]{2,0,1:T(8,128)(2,1)S(1)} collective-permute-done((bf16[384,2,384]{2,0,1:T(8,128)(2,1)S(1)}, bf16[384,2,384]{2,0,1:T(8,128)(2,1)S(1)}, u32[]{:S(2)}, u32[]{:S(2)}) %collective-permute-start.3) | collective-permute-done | bytes 589856 | tf_op jit(solution)/shard_map/while/body/eval_jaxpr/ppermute | solution.py:12
  833.6 23.7 %collective-permute-done.3 = bf16[384,2,384]{2,0,1:T(8,128)(2,1)S(1)} collective-permute-done((bf16[384,2,384]{2,0,1:T(8,128)(2,1)S(1)}, bf16[384,2,384]{2,0,1:T(8,128)(2,1)S(1)}, u32[]{:S(2)}, u32[]{:S(2)}) %collective-permute-start.3) | collective-permute-done | bytes 589856 | tf_op jit(solution)/shard_map/while/body/eval_jaxpr/ppermute | solution.py:12
  (261 shorter events, 339.3 us)
Async XLA Ops:
  41.2 29.0 %collective-permute-start.6 = (bf16[384,768]{1,0:T(8,128)(2,1)S(1)}, bf16[384,768]{1,0:T(8,128)(2,1)}, u32[]{:S(2)}, u32[]{:S(2)}) collective-permute-start(bf16[384,768]{1,0:T(8,128)(2,1)S(1)} %broadcast_select_fusion.3), channel_id=1, source_target_pairs={{32,0},{40,8},{48,16},{56,24},{64,32},{72,40},{80,48},{88,56},{96,... | collective-permute-start | bytes 1769480 | tf_op jit(solution)/shard_map/ppermute | solution.py:12
  43.8 25.5 %all-to-all-start.1 = ((bf16[48,2,8,384]{3,1,0,2:T(2,128)(2,1)}), bf16[48,2,8,384]{3,1,0,2:T(2,128)(2,1)S(1)}, u32[]{:S(2)}, u32[]{:S(2)}) async-start(bf16[48,2,8,384]{3,1,0,2:T(2,128)(2,1)} %copy.12), calls=%async_computation.1 | async-start | bytes 1179648 | tf_op jit(solution)/shard_map/all_to_all | solution.py:91
  71.4 25.6 %collective-permute-start.1 = (bf16[384,2,384]{2,0,1:T(8,128)(2,1)}, bf16[384,2,384]{2,0,1:T(8,128)(2,1)S(1)}, u32[]{:S(2)}, u32[]{:S(2)}) collective-permute-start(bf16[384,2,384]{2,0,1:T(8,128)(2,1)} %get-tuple-element.281), channel_id=1, source_target_pairs={{1,0},{2,1},{3,2},{4,3},{5,4},{6,5},{7,6},{0,7},{9,8},{10,9},{11,1... | collective-permute-start | bytes 1769480 | tf_op jit(solution)/shard_map/while/body/eval_jaxpr/ppermute | solution.py:12
  72.3 25.6 %collective-permute-start = (bf16[384,768]{1,0:T(8,128)(2,1)S(1)}, bf16[384,768]{1,0:T(8,128)(2,1)S(1)}, u32[]{:S(2)}, u32[]{:S(2)}) collective-permute-start(bf16[384,768]{1,0:T(8,128)(2,1)S(1)} %copy.29), channel_id=1, source_target_pairs={{8,0},{16,8},{24,16},{32,24},{40,32},{48,40},{56,48},{64,56},{72,6... | collective-permute-start | bytes 1769480 | tf_op jit(solution)/shard_map/while/body/eval_jaxpr/ppermute | solution.py:12
  98.0 25.6 %collective-permute-start = (bf16[384,768]{1,0:T(8,128)(2,1)S(1)}, bf16[384,768]{1,0:T(8,128)(2,1)S(1)}, u32[]{:S(2)}, u32[]{:S(2)}) collective-permute-start(bf16[384,768]{1,0:T(8,128)(2,1)S(1)} %copy.29), channel_id=1, source_target_pairs={{8,0},{16,8},{24,16},{32,24},{40,32},{48,40},{56,48},{64,56},{72,6... | collective-permute-start | bytes 1769480 | tf_op jit(solution)/shard_map/while/body/eval_jaxpr/ppermute | solution.py:12
  219.2 27.6 %collective-permute-start.1 = (bf16[384,2,384]{2,0,1:T(8,128)(2,1)}, bf16[384,2,384]{2,0,1:T(8,128)(2,1)S(1)}, u32[]{:S(2)}, u32[]{:S(2)}) collective-permute-start(bf16[384,2,384]{2,0,1:T(8,128)(2,1)} %get-tuple-element.281), channel_id=1, source_target_pairs={{1,0},{2,1},{3,2},{4,3},{5,4},{6,5},{7,6},{0,7},{9,8},{10,9},{11,1... | collective-permute-start | bytes 1769480 | tf_op jit(solution)/shard_map/while/body/eval_jaxpr/ppermute | solution.py:12
  219.2 28.5 %collective-permute-start = (bf16[384,768]{1,0:T(8,128)(2,1)S(1)}, bf16[384,768]{1,0:T(8,128)(2,1)S(1)}, u32[]{:S(2)}, u32[]{:S(2)}) collective-permute-start(bf16[384,768]{1,0:T(8,128)(2,1)S(1)} %copy.29), channel_id=1, source_target_pairs={{8,0},{16,8},{24,16},{32,24},{40,32},{48,40},{56,48},{64,56},{72,6... | collective-permute-start | bytes 1769480 | tf_op jit(solution)/shard_map/while/body/eval_jaxpr/ppermute | solution.py:12
  247.7 25.4 %collective-permute-start.1 = (bf16[384,2,384]{2,0,1:T(8,128)(2,1)}, bf16[384,2,384]{2,0,1:T(8,128)(2,1)S(1)}, u32[]{:S(2)}, u32[]{:S(2)}) collective-permute-start(bf16[384,2,384]{2,0,1:T(8,128)(2,1)} %get-tuple-element.281), channel_id=1, source_target_pairs={{1,0},{2,1},{3,2},{4,3},{5,4},{6,5},{7,6},{0,7},{9,8},{10,9},{11,1... | collective-permute-start | bytes 1769480 | tf_op jit(solution)/shard_map/while/body/eval_jaxpr/ppermute | solution.py:12
  247.8 26.3 %collective-permute-start = (bf16[384,768]{1,0:T(8,128)(2,1)S(1)}, bf16[384,768]{1,0:T(8,128)(2,1)S(1)}, u32[]{:S(2)}, u32[]{:S(2)}) collective-permute-start(bf16[384,768]{1,0:T(8,128)(2,1)S(1)} %copy.29), channel_id=1, source_target_pairs={{8,0},{16,8},{24,16},{32,24},{40,32},{48,40},{56,48},{64,56},{72,6... | collective-permute-start | bytes 1769480 | tf_op jit(solution)/shard_map/while/body/eval_jaxpr/ppermute | solution.py:12
  298.7 29.8 %collective-permute-start.1 = (bf16[384,2,384]{2,0,1:T(8,128)(2,1)}, bf16[384,2,384]{2,0,1:T(8,128)(2,1)S(1)}, u32[]{:S(2)}, u32[]{:S(2)}) collective-permute-start(bf16[384,2,384]{2,0,1:T(8,128)(2,1)} %get-tuple-element.281), channel_id=1, source_target_pairs={{1,0},{2,1},{3,2},{4,3},{5,4},{6,5},{7,6},{0,7},{9,8},{10,9},{11,1... | collective-permute-start | bytes 1769480 | tf_op jit(solution)/shard_map/while/body/eval_jaxpr/ppermute | solution.py:12
  298.7 30.7 %collective-permute-start = (bf16[384,768]{1,0:T(8,128)(2,1)S(1)}, bf16[384,768]{1,0:T(8,128)(2,1)S(1)}, u32[]{:S(2)}, u32[]{:S(2)}) collective-permute-start(bf16[384,768]{1,0:T(8,128)(2,1)S(1)} %copy.29), channel_id=1, source_target_pairs={{8,0},{16,8},{24,16},{32,24},{40,32},{48,40},{56,48},{64,56},{72,6... | collective-permute-start | bytes 1769480 | tf_op jit(solution)/shard_map/while/body/eval_jaxpr/ppermute | solution.py:12
  329.4 25.4 %collective-permute-start.1 = (bf16[384,2,384]{2,0,1:T(8,128)(2,1)}, bf16[384,2,384]{2,0,1:T(8,128)(2,1)S(1)}, u32[]{:S(2)}, u32[]{:S(2)}) collective-permute-start(bf16[384,2,384]{2,0,1:T(8,128)(2,1)} %get-tuple-element.281), channel_id=1, source_target_pairs={{1,0},{2,1},{3,2},{4,3},{5,4},{6,5},{7,6},{0,7},{9,8},{10,9},{11,1... | collective-permute-start | bytes 1769480 | tf_op jit(solution)/shard_map/while/body/eval_jaxpr/ppermute | solution.py:12
  329.5 26.3 %collective-permute-start = (bf16[384,768]{1,0:T(8,128)(2,1)S(1)}, bf16[384,768]{1,0:T(8,128)(2,1)S(1)}, u32[]{:S(2)}, u32[]{:S(2)}) collective-permute-start(bf16[384,768]{1,0:T(8,128)(2,1)S(1)} %copy.29), channel_id=1, source_target_pairs={{8,0},{16,8},{24,16},{32,24},{40,32},{48,40},{56,48},{64,56},{72,6... | collective-permute-start | bytes 1769480 | tf_op jit(solution)/shard_map/while/body/eval_jaxpr/ppermute | solution.py:12
  355.8 25.5 %collective-permute-start = (bf16[384,768]{1,0:T(8,128)(2,1)S(1)}, bf16[384,768]{1,0:T(8,128)(2,1)S(1)}, u32[]{:S(2)}, u32[]{:S(2)}) collective-permute-start(bf16[384,768]{1,0:T(8,128)(2,1)S(1)} %copy.29), channel_id=1, source_target_pairs={{8,0},{16,8},{24,16},{32,24},{40,32},{48,40},{56,48},{64,56},{72,6... | collective-permute-start | bytes 1769480 | tf_op jit(solution)/shard_map/while/body/eval_jaxpr/ppermute | solution.py:12
  381.4 25.4 %collective-permute-start = (bf16[384,768]{1,0:T(8,128)(2,1)S(1)}, bf16[384,768]{1,0:T(8,128)(2,1)S(1)}, u32[]{:S(2)}, u32[]{:S(2)}) collective-permute-start(bf16[384,768]{1,0:T(8,128)(2,1)S(1)} %copy.29), channel_id=1, source_target_pairs={{8,0},{16,8},{24,16},{32,24},{40,32},{48,40},{56,48},{64,56},{72,6... | collective-permute-start | bytes 1769480 | tf_op jit(solution)/shard_map/while/body/eval_jaxpr/ppermute | solution.py:12
  406.7 38.0 %collective-permute-start.1 = (bf16[384,2,384]{2,0,1:T(8,128)(2,1)}, bf16[384,2,384]{2,0,1:T(8,128)(2,1)S(1)}, u32[]{:S(2)}, u32[]{:S(2)}) collective-permute-start(bf16[384,2,384]{2,0,1:T(8,128)(2,1)} %get-tuple-element.281), channel_id=1, source_target_pairs={{1,0},{2,1},{3,2},{4,3},{5,4},{6,5},{7,6},{0,7},{9,8},{10,9},{11,1... | collective-permute-start | bytes 1769480 | tf_op jit(solution)/shard_map/while/body/eval_jaxpr/ppermute | solution.py:12
  406.8 39.0 %collective-permute-start = (bf16[384,768]{1,0:T(8,128)(2,1)S(1)}, bf16[384,768]{1,0:T(8,128)(2,1)S(1)}, u32[]{:S(2)}, u32[]{:S(2)}) collective-permute-start(bf16[384,768]{1,0:T(8,128)(2,1)S(1)} %copy.29), channel_id=1, source_target_pairs={{8,0},{16,8},{24,16},{32,24},{40,32},{48,40},{56,48},{64,56},{72,6... | collective-permute-start | bytes 1769480 | tf_op jit(solution)/shard_map/while/body/eval_jaxpr/ppermute | solution.py:12
  532.4 25.3 %collective-permute-start.3 = (bf16[384,2,384]{2,0,1:T(8,128)(2,1)S(1)}, bf16[384,2,384]{2,0,1:T(8,128)(2,1)S(1)}, u32[]{:S(2)}, u32[]{:S(2)}) collective-permute-start(bf16[384,2,384]{2,0,1:T(8,128)(2,1)S(1)} %get-tuple-element.302), channel_id=1, source_target_pairs={{1,0},{2,1},{3,2},{4,3},{5,4},{6,5},{7,6},{0,7},{9,8},{10,9},{11,1... | collective-permute-start | bytes 1769480 | tf_op jit(solution)/shard_map/while/body/eval_jaxpr/ppermute | solution.py:12
  532.5 25.3 %collective-permute-start.2 = (bf16[384,768]{1,0:T(8,128)(2,1)S(1)}, bf16[384,768]{1,0:T(8,128)(2,1)S(1)}, u32[]{:S(2)}, u32[]{:S(2)}) collective-permute-start(bf16[384,768]{1,0:T(8,128)(2,1)S(1)} %copy.41), channel_id=1, source_target_pairs={{8,0},{16,8},{24,16},{32,24},{40,32},{48,40},{56,48},{64,56},{72,6... | collective-permute-start | bytes 1769480 | tf_op jit(solution)/shard_map/while/body/eval_jaxpr/ppermute | solution.py:12
  558.0 24.8 %collective-permute-start.2 = (bf16[384,768]{1,0:T(8,128)(2,1)S(1)}, bf16[384,768]{1,0:T(8,128)(2,1)S(1)}, u32[]{:S(2)}, u32[]{:S(2)}) collective-permute-start(bf16[384,768]{1,0:T(8,128)(2,1)S(1)} %copy.41), channel_id=1, source_target_pairs={{8,0},{16,8},{24,16},{32,24},{40,32},{48,40},{56,48},{64,56},{72,6... | collective-permute-start | bytes 1769480 | tf_op jit(solution)/shard_map/while/body/eval_jaxpr/ppermute | solution.py:12
  606.6 29.0 %collective-permute-start.3 = (bf16[384,2,384]{2,0,1:T(8,128)(2,1)S(1)}, bf16[384,2,384]{2,0,1:T(8,128)(2,1)S(1)}, u32[]{:S(2)}, u32[]{:S(2)}) collective-permute-start(bf16[384,2,384]{2,0,1:T(8,128)(2,1)S(1)} %get-tuple-element.302), channel_id=1, source_target_pairs={{1,0},{2,1},{3,2},{4,3},{5,4},{6,5},{7,6},{0,7},{9,8},{10,9},{11,1... | collective-permute-start | bytes 1769480 | tf_op jit(solution)/shard_map/while/body/eval_jaxpr/ppermute | solution.py:12
  606.7 29.0 %collective-permute-start.2 = (bf16[384,768]{1,0:T(8,128)(2,1)S(1)}, bf16[384,768]{1,0:T(8,128)(2,1)S(1)}, u32[]{:S(2)}, u32[]{:S(2)}) collective-permute-start(bf16[384,768]{1,0:T(8,128)(2,1)S(1)} %copy.41), channel_id=1, source_target_pairs={{8,0},{16,8},{24,16},{32,24},{40,32},{48,40},{56,48},{64,56},{72,6... | collective-permute-start | bytes 1769480 | tf_op jit(solution)/shard_map/while/body/eval_jaxpr/ppermute | solution.py:12
  635.8 25.1 %collective-permute-start.3 = (bf16[384,2,384]{2,0,1:T(8,128)(2,1)S(1)}, bf16[384,2,384]{2,0,1:T(8,128)(2,1)S(1)}, u32[]{:S(2)}, u32[]{:S(2)}) collective-permute-start(bf16[384,2,384]{2,0,1:T(8,128)(2,1)S(1)} %get-tuple-element.302), channel_id=1, source_target_pairs={{1,0},{2,1},{3,2},{4,3},{5,4},{6,5},{7,6},{0,7},{9,8},{10,9},{11,1... | collective-permute-start | bytes 1769480 | tf_op jit(solution)/shard_map/while/body/eval_jaxpr/ppermute | solution.py:12
  635.9 25.1 %collective-permute-start.2 = (bf16[384,768]{1,0:T(8,128)(2,1)S(1)}, bf16[384,768]{1,0:T(8,128)(2,1)S(1)}, u32[]{:S(2)}, u32[]{:S(2)}) collective-permute-start(bf16[384,768]{1,0:T(8,128)(2,1)S(1)} %copy.41), channel_id=1, source_target_pairs={{8,0},{16,8},{24,16},{32,24},{40,32},{48,40},{56,48},{64,56},{72,6... | collective-permute-start | bytes 1769480 | tf_op jit(solution)/shard_map/while/body/eval_jaxpr/ppermute | solution.py:12
  (44 other events, 956.4 us)
where the time goes:
time: 881 us; the launch traced here: 880 us
  waiting for transfers between devices  782 us (89%)
  matrix products  38.3 us (4%)
  other arithmetic  21.9 us (2%)
  blocking collectives  14.8 us (2%)
  starting transfers between devices  14.2 us (2%)
    ppermute x66, waiting for transfers between devices, shifted(): return lax.ppermute(block, axis, route)  765 us
    dot_general x30, matrix products, one_group(): jnp.dot(fetch(state, group * inner + 0, 0), right_now, preferred_element_...  35.5 us
  transfers between devices with their start and end apart: 67, of which 36 were waited for; matrix products, arithmetic and copies ran while one was open for 6% of the time, Pallas kernels for 0%

commit v1 on v0

v1 whole, which is shorter than its diff:
```python
import jax
import jax.numpy as jnp
from jax import lax
from jax.sharding import PartitionSpec as P

BLK = 128


def tile_mask(mask, row_id, col_id, rows, width):
    row_blocks = rows // BLK
    col_blocks = width // BLK
    small = lax.dynamic_slice(
        mask, (row_id * row_blocks, col_id * col_blocks), (row_blocks, col_blocks)
    ).astype(jnp.float32)
    return jnp.broadcast_to(small[:, None, :, None], (row_blocks, BLK, col_blocks, BLK)).reshape(
        rows, width
    )


def on_device(density, pattern, filter_square, filter_cube):
    row_count = lax.axis_size("row")
    col_count = lax.axis_size("col")
    row_id = lax.axis_index("row")
    col_id = lax.axis_index("col")
    rows_one, order = density.shape
    nblocks = pattern.shape[0]
    rows = order // row_count
    width = order // col_count
    first = (row_id * col_count + col_id) * rows_one
    block_of = (first + jnp.arange(rows_one, dtype=jnp.int32)) // BLK
    row_mask = jnp.take(pattern, block_of, axis=0).astype(jnp.bfloat16)
    full_mask = jnp.broadcast_to(row_mask[:, :, None], (rows_one, nblocks, BLK)).reshape(
        rows_one, order
    )
    local = density * full_mask
    left = lax.all_gather(local, "col", axis=0, tiled=True)
    tile = lax.dynamic_slice(left, (0, col_id * width), (rows, width))
    right = lax.all_gather(tile, "row", axis=0, tiled=True)
    square = jnp.dot(left, right, preferred_element_type=jnp.float32)
    square = square * tile_mask(filter_square, row_id, col_id, rows, width)
    half = lax.all_gather(square.astype(jnp.bfloat16), "row", axis=0, tiled=True)
    cube = jnp.dot(left, half, preferred_element_type=jnp.float32)
    cube = cube * tile_mask(filter_cube, row_id, col_id, rows, width)
    return 3.0 * square - 2.0 * cube


def solution(mesh):
    placed = (P(("row", "col"), None), P(), P(), P())
    return jax.shard_map(
        on_device, mesh=mesh, in_specs=placed, out_specs=P("row", "col"), check_vma=False
    )
```

time: 881 us -> 232 us (0.26)
  the two profiles are of different devices: /device:TPU:126 before, /device:TPU:1 now
where the time goes in v1:
time: 232 us
  waiting for transfers between devices  192 us (83%)
  matrix products  19.9 us (9%)
  between operations  13.2 us (6%)
  local copies, waits for them, and re-layouts  3.89 us (2%)
  other arithmetic  2.93 us (1%)
    all_gather x1, waiting for transfers between devices, on_device(): left = lax.all_gather(local, 'col', axis=0, tiled=True)  78.9 us
    all_gather x1, waiting for transfers between devices, on_device(): lax.all_gather(square.astype(jnp.bfloat16), 'row', axis=0, tiled=True)  58.1 us
    all_gather x1, waiting for transfers between devices, on_device(): right = lax.all_gather(tile, 'row', axis=0, tiled=True)  54.9 us
    dot_general x1, matrix products, on_device(): cube = jnp.dot(left, half, preferred_element_type=jnp.float32)  10.1 us
    dot_general x1, matrix products, on_device(): square = jnp.dot(left, right, preferred_element_type=jnp.float32)  9.77 us
  transfers between devices with their start and end apart: 3, of which 3 were waited for; matrix products, arithmetic and copies ran while one was open for 0% of the time, Pallas kernels for 0%

profile of v1, /device:TPU:1, one launch (start us, length us, event | category | flops | bytes accessed | tf_op | source)
XLA Modules:
  0.0 231.8 jit_solution(9919951318664396545)
XLA Ops:
  6.5 0.0 copy-start
  6.5 0.0 all-gather.4.cloned.1.call-start
  6.6 0.7 copy-done
  7.3 0.6 gather_fusion
  7.9 0.1 select_convert_fusion
  7.9 0.4 broadcast_in_dim.30
  8.3 2.0 bitcast_multiply_fusion
  10.3 0.0 all-gather.4.cloned.1.call-update
  10.4 0.0 all-gather.6.cloned.1.call-start
  10.4 78.9 %all-gather.4.cloned.1.call-done = bf16[384,6144]{1,0:T(8,128)(2,1)} async-done(((bf16[48,6144]{1,0:T(8,128)(2,1)}), bf16[384,6144]{1,0:T(8,128)(2,1)}) %all-gather.4.cloned.1.call-update) | async-done | bytes 4718608 | tf_op jit(solution)/shard_map/all_gather | solution.py:36
  89.3 1.9 constant_dynamic-slice_fusion
  91.2 0.0 all-gather.6.cloned.1.call-update
  91.2 0.0 all-gather.8.cloned.1.call-start
  91.3 0.8 dynamic-slice_convert_fusion
  92.1 54.9 %all-gather.6.cloned.1.call-done = bf16[6144,768]{1,0:T(8,128)(2,1)} async-done(((bf16[384,768]{1,0:T(8,128)(2,1)}), bf16[6144,768]{1,0:T(8,128)(2,1)}) %all-gather.6.cloned.1.call-update) | async-done | bytes 9437200 | tf_op jit(solution)/shard_map/all_gather | solution.py:38
  146.9 0.2 broadcast_in_dim.31
  147.1 9.8 %fusion.3 = (bf16[384,768]{1,0:T(8,128)(2,1)}, f32[384,768]{1,0:T(8,128)S(1)}) fusion(f32[48,8,6,128]{3,2,1,0:T(8,128)S(1)} %bitcast.18, bf16[384,6144]{1,0:T(8,128)(2,1)} %all-gather.4.cloned.1.call-done, bf16[6144,768]{1,0:T(8,128)(2,1)} %all-gather.6.cloned.1.call-done), kind=kOutput, calls=%fused_computation.23 | convolution fusion | flops 3624468480 | bytes 17104896 | tf_op jit(solution)/shard_map/dot_general | solution.py:39
  156.9 0.0 all-gather.8.cloned.1.call-update
  156.9 58.1 %all-gather.8.cloned.1.call-done = bf16[6144,768]{1,0:T(8,128)(2,1)} async-done(((bf16[384,768]{1,0:T(8,128)(2,1)}), bf16[6144,768]{1,0:T(8,128)(2,1)}) %all-gather.8.cloned.1.call-update) | async-done | bytes 9437200 | tf_op jit(solution)/shard_map/all_gather | solution.py:41
  215.0 0.2 broadcast_in_dim.32
  215.1 10.1 %fusion.1 = f32[384,768]{1,0:T(8,128)} fusion(bf16[384,6144]{1,0:T(8,128)(2,1)} %all-gather.4.cloned.1.call-done, bf16[6144,768]{1,0:T(8,128)(2,1)} %all-gather.8.cloned.1.call-done, f32[48,8,6,128]{3,2,1,0:T(8,128)S(1)} %bitcast.19, f32[384,768]{1,0:T(8,128)S(1)} %get-tuple-element.6), kind=kOutput, calls=%fused_computation.4 | convolution fusion | flops 3625058304 | bytes 17694720 | tf_op jit(solution)/shard_map/dot_general | solution.py:42
  (3 shorter events, 0.0 us)
Async XLA Ops:
  6.5 0.7 copy-start
  6.5 82.7 %all-gather.4.cloned.1.call-start = ((), (), s32[]{:S(2)}) async-start(), calls=%async_computation | async-start | bytes 5308416 | tf_op jit(solution)/shard_map/all_gather | solution.py:36
  10.4 136.6 %all-gather.6.cloned.1.call-start = ((), (), s32[]{:S(2)}) async-start(), calls=%async_computation.1 | async-start | bytes 10027008 | tf_op jit(solution)/shard_map/all_gather | solution.py:38
  91.2 123.7 %all-gather.8.cloned.1.call-start = ((), (), s32[]{:S(2)}) async-start(), calls=%async_computation.2 | async-start | bytes 10027008 | tf_op jit(solution)/shard_map/all_gather | solution.py:41
Sparse Core Ops, SparseCore 0:
  10.5 78.7 all-gather.3
  91.3 55.5 all-gather.5
  157.0 57.8 all-gather.7

commit v2 on v1

v2 whole, which is shorter than its diff:
```python
import functools

import jax
import jax.numpy as jnp
from jax import lax
from jax.experimental import pallas as pl
from jax.experimental.pallas import tpu as pltpu
from jax.sharding import PartitionSpec as P

BLK = 128
XS, ZS = 4, 4
MESH = pl.DeviceIdType.MESH
SEMS = 96


def kernel(cuts, x_ref, m_ref, f2_ref, f3_ref, o_ref, left, right, half, square, ss, rs):
    rows_one, order = x_ref.shape
    rows, width = o_ref.shape
    pair = 2 * rows
    part = width // cuts
    row_id = lax.axis_index("row")
    col_id = lax.axis_index("col")
    core, x, ylo = row_id % 2, row_id // 2 % XS, row_id // (2 * XS)
    z, yhi = col_id % ZS, col_id // ZS

    def at(dx=0, dyl=0, dyh=0, dz=0, dc=0):
        row = (ylo + dyl) % 2 * (2 * XS) + (x + dx + XS) % XS * 2 + (core + dc) % 2
        col = (yhi + dyh) % 2 * ZS + (z + dz + ZS) % ZS
        return (row, col)

    names = {}
    started = []

    def number(name):
        return names.setdefault(name, len(names))

    def send(name, src, dst, target):
        k = number(name)
        copy = pltpu.make_async_remote_copy(
            src_ref=src,
            dst_ref=dst,
            send_sem=ss.at[k],
            recv_sem=rs.at[k],
            device_id=target,
            device_id_type=MESH,
        )
        copy.start()
        started.append(copy)

    def receive(name, landing):
        k = number(name)
        pltpu.make_async_remote_copy(
            src_ref=landing,
            dst_ref=landing,
            send_sem=ss.at[k],
            recv_sem=rs.at[k],
            device_id=at(dc=1),
            device_id_type=MESH,
        ).wait_recv()

    exchange = [(dyh, dz) for dyh in range(2) for dz in range(ZS) if dyh or dz]
    partners = [at(dyh=dyh, dz=dz) for dyh, dz in exchange]
    partners += [at(dx=1), at(dx=-1), at(dyl=1), at(dc=1)]
    barrier = pltpu.get_barrier_semaphore()
    for device in partners:
        pl.semaphore_signal(barrier, inc=1, device_id=device, device_id_type=MESH)

    def piece(col):
        return pl.ds(pl.multiple_of(col * rows_one, 16), rows_one)

    def columns(col):
        return pl.ds(pl.multiple_of(col * width, 128), width)

    for g in range(rows_one // 16):
        at_row = pl.multiple_of(col_id * rows_one + 16 * g, 16)
        left[pl.ds(at_row, 16), :] = (
            x_ref[16 * g : 16 * g + 16, :].astype(jnp.float32) * m_ref[g : g + 1, :]
        ).astype(jnp.bfloat16)
    pl.semaphore_wait(barrier, len(partners))

    def tile(buf, dyl=0, dx=0, dc=0, part_of=None):
        c = (core + dc) % 2
        q = (ylo + dyl) % 2 * XS + (x + dx + XS) % XS
        size = rows if part_of is None else rows // 2
        start = c * rows + (0 if part_of is None else part_of * size)
        return buf.at[q, pl.ds(pl.multiple_of(start, 16), size), :]

    for dyh, dz in exchange:
        device = at(dyh=dyh, dz=dz)
        send(
            ("grid", dyh, dz),
            left.at[piece(col_id), columns(device[1])],
            tile(right).at[piece(col_id), :],
            device,
        )
    own = ylo * XS + x
    right[own, pl.ds(pl.multiple_of(core * rows + col_id * rows_one, 16), rows_one), :] = left[
        piece(col_id), columns(col_id)
    ]
    for dyh, dz in exchange:
        source = at(dyh=dyh, dz=-dz)
        receive(("grid", dyh, dz), tile(right).at[piece(source[1]), :])

    class Gather:
        def __init__(self, name, buf, y_first):
            self.name, self.buf, self.y_first = name, buf, y_first

        def put(self, what, target, **where):
            ref = tile(self.buf, **where)
            send((self.name, what), ref, ref, target)

        def get(self, what, **where):
            receive((self.name, what), tile(self.buf, **where))

        def begin(self):
            self.put("x+0", at(dx=1))
            self.put("x-0", at(dx=-1))
            self.put("y0", at(dyl=1))
            self.put("c00", at(dc=1))

        def turn(self):
            self.get("y0", dyl=1)
            self.put("x+1", at(dx=1), dyl=1)
            self.put("x-1", at(dx=-1), dyl=1)
            self.put("c10", at(dc=1), dyl=1)

        def near(self, dyl):
            self.get(f"x+{dyl}", dyl=dyl, dx=-1)
            self.put(f"f+{dyl}", at(dx=1), dyl=dyl, dx=-1, part_of=0)
            self.get(f"x-{dyl}", dyl=dyl, dx=1)
            self.put(f"f-{dyl}", at(dx=-1), dyl=dyl, dx=1, part_of=1)
            for dx in (-1, 1):
                self.put(f"c{dyl}{dx}", at(dc=1), dyl=dyl, dx=dx)
                if not self.y_first:
                    self.put(f"y{dx}", at(dyl=1), dx=dx)

        def far(self, dyl):
            self.get(f"f+{dyl}", dyl=dyl, dx=-2, part_of=0)
            self.get(f"f-{dyl}", dyl=dyl, dx=2, part_of=1)
            self.put(f"c{dyl}2", at(dc=1), dyl=dyl, dx=2)
            if not self.y_first:
                self.put("y2", at(dyl=1), dx=2)

        def across(self, dx):
            self.get(f"y{dx}", dyl=1, dx=dx)
            self.put(f"c1{dx}", at(dc=1), dyl=1, dx=dx)

        def sibling(self, dyl, dx):
            self.get(f"c{dyl}{dx}", dyl=dyl, dx=dx, dc=1)

    panel = Gather("right", right, True)
    panel.begin()

    def lrows(dyh=0, dz=0, h=None):
        row = left.at[piece(at(dyh=dyh, dz=dz)[1])]
        return row if h is None else row.at[:, pl.ds(h * (order // 2), order // 2)]

    def lput(what, target, **where):
        ref = lrows(**where)
        send(("left", what), ref, ref, target)

    lput("z+0", at(dz=1))
    lput("z-0", at(dz=-1))
    lput("q", at(dyh=1))
    panel.near(0)
    receive(("left", "z+0"), lrows(dz=-1))
    lput("f+0", at(dz=1), dz=-1, h=0)
    receive(("left", "z-0"), lrows(dz=1))
    lput("f-0", at(dz=-1), dz=1, h=1)
    panel.turn()
    receive(("left", "q"), lrows(dyh=1))
    lput("z+1", at(dz=1), dyh=1)
    lput("z-1", at(dz=-1), dyh=1)
    panel.far(0)
    panel.near(1)
    receive(("left", "z+1"), lrows(dyh=1, dz=-1))
    lput("f+1", at(dz=1), dyh=1, dz=-1, h=0)
    receive(("left", "z-1"), lrows(dyh=1, dz=1))
    lput("f-1", at(dz=-1), dyh=1, dz=1, h=1)
    panel.far(1)
    for dyh in range(2):
        receive(("left", f"f+{dyh}"), lrows(dyh=dyh, dz=-2, h=0))
        receive(("left", f"f-{dyh}"), lrows(dyh=dyh, dz=2, h=1))
    for dyl in range(2):
        for dx in (0, -1, 1, 2):
            panel.sibling(dyl, dx)

    pairs = order // pair

    def depth(k):
        return pl.ds(pl.multiple_of(k * pair, 128), pair)

    def square_part(n):
        at_cols = slice(n * part, (n + 1) * part)
        square[:, at_cols] = jnp.dot(
            left[:, 0:pair], right[0, :, at_cols], preferred_element_type=jnp.float32
        )

        def step(k, carry):
            square[:, at_cols] += jnp.dot(
                left[:, depth(k)], right[k, :, at_cols], preferred_element_type=jnp.float32
            )
            return carry

        lax.fori_loop(1, pairs, step, 0)
        for b in range(rows // BLK):
            at_rows = slice(b * BLK, (b + 1) * BLK)
            kept = square[at_rows, at_cols] * f2_ref[b : b + 1, at_cols]
            square[at_rows, at_cols] = kept
            half[
                n, own, pl.ds(pl.multiple_of(core * rows + b * BLK, 16), BLK), :
            ] = kept.astype(jnp.bfloat16)

    def cube_dot(n, dyl, dx, first=False):
        at_cols = slice(n * part, (n + 1) * part)
        k = (ylo + dyl) % 2 * XS + (x + dx + XS) % XS
        value = jnp.dot(left[:, depth(k)], half[n, k], preferred_element_type=jnp.float32)
        if first:
            o_ref[:, at_cols] = value
        else:
            o_ref[:, at_cols] += value

    def cube_part(n):
        at_cols = slice(n * part, (n + 1) * part)
        o_ref[:, at_cols] = jnp.dot(
            left[:, 0:pair], half[n, 0], preferred_element_type=jnp.float32
        )

        def step(k, carry):
            o_ref[:, at_cols] += jnp.dot(
                left[:, depth(k)], half[n, k], preferred_element_type=jnp.float32
            )
            return carry

        lax.fori_loop(1, pairs, step, 0)

    def finish(n):
        at_cols = slice(n * part, (n + 1) * part)
        for b in range(rows // BLK):
            at_rows = slice(b * BLK, (b + 1) * BLK)
            cube = o_ref[at_rows, at_cols] * f3_ref[b : b + 1, at_cols]
            o_ref[at_rows, at_cols] = 3.0 * square[at_rows, at_cols] - 2.0 * cube

    gathers = [Gather(f"half{n}", half.at[n], n > 0) for n in range(cuts)]
    a, b, c = gathers
    square_part(0)
    a.begin()
    square_part(1)
    b.begin()
    a.near(0)
    square_part(2)
    c.begin()
    b.turn()
    a.far(0)
    a.across(0)
    b.near(0)
    c.turn()
    b.near(1)
    a.across(-1)
    a.across(1)
    c.near(0)
    b.far(0)
    c.near(1)
    b.far(1)
    a.across(2)
    for dyl in range(2):
        for dx in (0, -1, 1, 2):
            a.sibling(dyl, dx)
    cube_part(0)
    finish(0)
    for dyl in range(2):
        for dx in (0, -1, 1, 2):
            b.sibling(dyl, dx)
    cube_part(1)
    finish(1)
    for dyl in range(2):
        for dx in (0, -1, 1):
            c.sibling(dyl, dx)
            cube_dot(2, dyl, dx, first=dyl == 0 and dx == 0)
    c.far(0)
    c.far(1)
    for dyl in range(2):
        c.sibling(dyl, 2)
        cube_dot(2, dyl, 2)
    finish(2)
    for copy in started:
        copy.wait_send()


def on_device(density, pattern, filter_square, filter_cube):
    row_count = lax.axis_size("row")
    col_count = lax.axis_size("col")
    row_id = lax.axis_index("row")
    col_id = lax.axis_index("col")
    rows_one, order = density.shape
    rows = order // row_count
    width = order // col_count
    cuts = 3

    def expanded(mask, row, col, height, cols):
        small = lax.dynamic_slice(mask, (row, col), (height, cols)).astype(jnp.float32)
        return jnp.repeat(small, BLK, axis=1)

    def tile_rows(mask):
        return expanded(
            mask, row_id * (rows // BLK), col_id * (width // BLK), rows // BLK, width // BLK
        )

    groups = rows_one // 16
    first = (row_id * col_count + col_id) * rows_one
    block_of = (first + 16 * jnp.arange(groups, dtype=jnp.int32)) // BLK
    kept = jnp.repeat(jnp.take(pattern, block_of, axis=0).astype(jnp.float32), BLK, axis=1)
    pairs = order // (2 * rows)
    vmem = pl.BlockSpec(memory_space=pltpu.VMEM)
    return pl.pallas_call(
        functools.partial(kernel, cuts),
        out_shape=jax.ShapeDtypeStruct((rows, width), jnp.float32),
        in_specs=[vmem] * 4,
        out_specs=vmem,
        scratch_shapes=[
            pltpu.VMEM((rows, order), jnp.bfloat16),
            pltpu.VMEM((pairs, 2 * rows, width), jnp.bfloat16),
            pltpu.VMEM((cuts, pairs, 2 * rows, width // cuts), jnp.bfloat16),
            pltpu.VMEM((rows, width), jnp.float32),
            pltpu.SemaphoreType.DMA((SEMS,)),
            pltpu.SemaphoreType.DMA((SEMS,)),
        ],
        compiler_params=pltpu.CompilerParams(
            collective_id=0, has_side_effects=True, vmem_limit_bytes=48 << 20
        ),
    )(density, kept, tile_rows(filter_square), tile_rows(filter_cube))


def solution(mesh):
    placed = (P(("row", "col"), None), P(), P(), P())
    return jax.shard_map(
        on_device, mesh=mesh, in_specs=placed, out_specs=P("row", "col"), check_vma=False
    )
```

time: 232 us -> 114 us (0.49)
  waiting for transfers between devices: 192 us -> 0 us
  Pallas kernels: 0 us -> 110 us
  matrix products: 19.9 us -> 0 us
  between operations: 13.2 us -> 0.05 us
    all_gather x3 -> x0, waiting for transfers between devices: 192 us -> none  [the longest x1 78.9 us: on_device(): left = lax.all_gather(local, 'col', axis=0, tiled=True)]
    pallas_call x0 -> x1, Pallas kernels: none -> 110 us  [on_device(): pl.pallas_call(functools.partial(kernel, cuts), out_shape=jax.ShapeDtypeS...]
    dot_general x2 -> x0, matrix products: 19.9 us -> none  [the longest x1 10.1 us: on_device(): cube = jnp.dot(left, half, preferred_element_type=jnp.float32)]
  transfers between devices with their start and end apart: 3 -> 0, of which waited for: 3 -> 0; matrix products, arithmetic and copies ran while one was open for 0% -> 0% of each run, Pallas kernels for 0% -> 0%
where the time goes in v2:
time: 114 us
  Pallas kernels  110 us (96%)
  local copies, waits for them, and re-layouts  2.91 us (3%)
    pallas_call x1, Pallas kernels, on_device(): pl.pallas_call(functools.partial(kernel, cuts), out_shape=jax.ShapeDtypeS...  110 us
    unnamed x11, local copies, waits for them, and re-layouts  2.35 us

profile of v2, /device:TPU:1, one launch (start us, length us, event | category | flops | bytes accessed | tf_op | source)
XLA Modules:
  0.0 114.0 jit_solution(8083883274528395959)
XLA Ops:
  0.0 0.0 copy-start
  0.0 0.8 dynamic-slice_convert_fusion
  0.8 0.0 copy-done
  0.9 0.6 gather_fusion
  1.4 0.1 select_convert_fusion
  1.5 0.1 broadcast_bitcast_fusion.1
  1.6 0.1 broadcast_bitcast_fusion.2
  1.6 0.1 broadcast_bitcast_fusion
  1.8 0.0 copy-start.1
  1.8 1.1 copy-done.1
  2.8 110.1 %shard_map.46 = f32[384,768]{1,0:T(8,128)S(1)} custom-call(bf16[48,6144]{1,0:T(8,128)(2,1)S(1)} %copy-done.1, f32[3,6144]{1,0:T(4,128)S(1)} %bitcast.17, f32[3,768]{1,0:T(4,128)S(1)} %bitcast.19, f32[3,768]{1,0:T(4,128)S(1)} %bitcast.18), custom_call_target="tpu_custom_call" | custom-call | tf_op jit(solution)/shard_map/pallas_call | solution.py:315
  113.0 1.0 copy.15
  (6 shorter events, 0.1 us)
Async XLA Ops:
  0.0 0.8 copy-start
  1.8 1.1 copy-start.1

commit v3 on v2

v3 whole, which is shorter than its diff:
```python
import functools

import jax
import jax.numpy as jnp
from jax import lax
from jax.experimental import pallas as pl
from jax.experimental.pallas import tpu as pltpu
from jax.sharding import PartitionSpec as P

BLK = 128
XS, ZS = 4, 4
MESH = pl.DeviceIdType.MESH
SEMS = 128


def kernel(cuts, d_ref, p_ref, f2_ref, f3_ref, out, mine, o_ref, left, right, half, square, keep, keep2,
           keep3, ls, ss, rs):
    rows_one, order = d_ref.shape
    rows, width = o_ref.shape
    pair = 2 * rows
    part = width // cuts
    row_id = lax.axis_index("row")
    col_id = lax.axis_index("col")
    core, x, ylo = row_id % 2, row_id // 2 % XS, row_id // (2 * XS)
    z, yhi = col_id % ZS, col_id // ZS

    def at(dx=0, dyl=0, dyh=0, dz=0, dc=0):
        row = (ylo + dyl) % 2 * (2 * XS) + (x + dx + XS) % XS * 2 + (core + dc) % 2
        col = (yhi + dyh) % 2 * ZS + (z + dz + ZS) % ZS
        return (row, col)

    names = {}
    started = []

    def number(name):
        return names.setdefault(name, len(names))

    def send(name, src, dst, target):
        k = number(name)
        copy = pltpu.make_async_remote_copy(
            src_ref=src,
            dst_ref=dst,
            send_sem=ss.at[k],
            recv_sem=rs.at[k],
            device_id=target,
            device_id_type=MESH,
        )
        copy.start()
        started.append(copy)

    def receive(name, landing):
        k = number(name)
        pltpu.make_async_remote_copy(
            src_ref=landing,
            dst_ref=landing,
            send_sem=ss.at[k],
            recv_sem=rs.at[k],
            device_id=at(dc=1),
            device_id_type=MESH,
        ).wait_recv()

    def settle(count):
        for _ in range(count):
            started.pop(0).wait_send()

    fetches = [
        pltpu.make_async_copy(src, dst, ls.at[k])
        for k, (src, dst) in enumerate(
            ((d_ref, mine), (p_ref, keep), (f2_ref, keep2), (f3_ref, keep3))
        )
    ]
    for fetch in fetches:
        fetch.start()
    partners = [at(dz=dz) for dz in range(1, ZS)]
    partners += [at(dx=1), at(dx=-1), at(dyl=1), at(dyh=1), at(dc=1)]
    barrier = pltpu.get_barrier_semaphore()
    for device in partners:
        pl.semaphore_signal(barrier, inc=1, device_id=device, device_id_type=MESH)
    for fetch in fetches:
        fetch.wait()

    def piece(col):
        return pl.ds(pl.multiple_of(col * rows_one, 16), rows_one)

    def columns(col):
        return pl.ds(pl.multiple_of(col * width, 128), width)

    first = (row_id * (order // width) + col_id) * rows_one
    for g in range(rows_one // 16):
        at_row = pl.multiple_of(col_id * rows_one + 16 * g, 16)
        block = (first + 16 * g) // BLK
        for k in range(order // BLK):
            cols = slice(k * BLK, (k + 1) * BLK)
            left[pl.ds(at_row, 16), cols] = (
                mine[16 * g : 16 * g + 16, cols].astype(jnp.float32)
                * keep[block, k].astype(jnp.float32)
            ).astype(jnp.bfloat16)
    pl.semaphore_wait(barrier, len(partners))

    def tile(buf, dyl=0, dx=0, dc=0, cut=None):
        c = (core + dc) % 2
        q = (ylo + dyl) % 2 * XS + (x + dx + XS) % XS
        number_of, of = cut or (0, 1)
        size = rows // of
        return buf.at[q, pl.ds(pl.multiple_of(c * rows + number_of * size, 16), size), :]

    class Gather:
        def __init__(self, name, buf, y_first, halved=None):
            self.name, self.buf, self.y_first, self.halved = name, buf, y_first, halved

        def view(self, part_of=None, **where):
            if self.halved is None:
                cut = None if part_of is None else (part_of, 2)
            elif part_of is None:
                cut = (self.halved, 2)
            else:
                cut = (2 * self.halved + part_of, 4)
            return tile(self.buf, cut=cut, **where)

        def put(self, what, target, **where):
            ref = self.view(**where)
            send((self.name, what), ref, ref, target)

        def get(self, what, **where):
            receive((self.name, what), self.view(**where))

        def begin(self):
            self.put("x+0", at(dx=1))
            self.put("x-0", at(dx=-1))
            self.put("y0", at(dyl=1))
            self.put("c00", at(dc=1))

        def turn(self):
            self.get("y0", dyl=1)
            self.put("x+1", at(dx=1), dyl=1)
            self.put("x-1", at(dx=-1), dyl=1)
            self.put("c10", at(dc=1), dyl=1)

        def near(self, dyl):
            self.get(f"x+{dyl}", dyl=dyl, dx=-1)
            self.put(f"f+{dyl}", at(dx=1), dyl=dyl, dx=-1, part_of=0)
            self.get(f"x-{dyl}", dyl=dyl, dx=1)
            self.put(f"f-{dyl}", at(dx=-1), dyl=dyl, dx=1, part_of=1)
            for dx in (-1, 1):
                if not self.y_first:
                    self.put(f"y{dx}", at(dyl=1), dx=dx)
                self.put(f"c{dyl}{dx}", at(dc=1), dyl=dyl, dx=dx)

        def far(self, dyl):
            self.get(f"f+{dyl}", dyl=dyl, dx=-2, part_of=0)
            self.get(f"f-{dyl}", dyl=dyl, dx=2, part_of=1)
            if not self.y_first:
                self.put("y2", at(dyl=1), dx=2)
            self.put(f"c{dyl}2", at(dc=1), dyl=dyl, dx=2)

        def across(self, dx):
            self.get(f"y{dx}", dyl=1, dx=dx)
            self.put(f"c1{dx}", at(dc=1), dyl=1, dx=dx)

        def sibling(self, dyl, dx):
            self.get(f"c{dyl}{dx}", dyl=dyl, dx=dx, dc=1)

    spans = {
        "most": (lambda h: (1 - h) * (order // 4), 3 * order // 4),
        "far": (lambda h: (1 - h) * (order // 2), order // 2),
        "mid": (lambda h: (1 + h) * (order // 4), order // 4),
        "last": (lambda h: h * (3 * order // 4), order // 4),
    }

    def lrows(span, dyh=0, dz=0, part_of=None):
        begin, size = spans[span]
        begin = begin((yhi + dyh) % 2)
        if part_of is not None:
            size = size // 2
            begin = begin + part_of * size
        return left.at[piece(at(dyh=dyh, dz=dz)[1]), pl.ds(pl.multiple_of(begin, 128), size)]

    def lput(what, span, target, **where):
        ref = lrows(span, **where)
        send(("left", what, span), ref, ref, target)

    def lget(what, span, **where):
        receive(("left", what, span), lrows(span, **where))

    def lbegin(span, dyh):
        lput("z+", span, at(dz=1), dyh=dyh)
        lput("z-", span, at(dz=-1), dyh=dyh)

    def lnear(span, dyh):
        lget("z+", span, dyh=dyh, dz=-1)
        lput("f+", span, at(dz=1), dyh=dyh, dz=-1, part_of=0)
        lget("z-", span, dyh=dyh, dz=1)
        lput("f-", span, at(dz=-1), dyh=dyh, dz=1, part_of=1)

    def lfar(span, dyh):
        lget("f+", span, dyh=dyh, dz=-2, part_of=0)
        lget("f-", span, dyh=dyh, dz=2, part_of=1)

    own = ylo * XS + x

    def own_rows(source):
        start = pl.multiple_of(core * rows + source * rows_one, 16)
        return right.at[own, pl.ds(start, rows_one), :]

    def grid_begin(dyh):
        source = at(dyh=dyh)[1]
        for dz in (1, 3, 2):
            device = at(dz=dz)
            block = left.at[piece(source), columns(device[1])]
            send(("grid", dyh, dz), block, own_rows(source), device)
        own_rows(source)[...] = left[piece(source), columns(col_id)]

    def grid_end(dyh):
        for dz in (1, 3, 2):
            receive(("grid", dyh, dz), own_rows(at(dyh=dyh, dz=-dz)[1]))

    a = Gather("right0", right, True, yhi)
    b = Gather("right1", right, True, (yhi + 1) % 2)
    grid_begin(0)
    lput("q", "far", at(dyh=1))
    settle(3)
    lbegin("last", 0)
    grid_end(0)
    a.begin()
    lget("q", "far", dyh=1)
    grid_begin(1)
    lput("q", "mid", at(dyh=1))
    lbegin("most", 0)
    lbegin("far", 1)
    lnear("last", 0)
    a.near(0)
    a.turn()
    grid_end(1)
    b.begin()
    lget("q", "mid", dyh=1)
    lbegin("mid", 1)
    a.far(0)
    a.near(1)
    b.turn()
    b.near(0)
    for dz in (0, 1, -1):
        lput(f"w{dz}", "last", at(dyh=1), dz=dz)
    lnear("most", 0)
    lfar("last", 0)
    lput("w2", "last", at(dyh=1), dz=2)
    lnear("far", 1)
    lnear("mid", 1)
    a.far(1)
    b.near(1)
    b.far(0)
    b.far(1)
    lfar("most", 0)
    lfar("far", 1)
    lfar("mid", 1)
    for dz in (0, 1, -1, 2):
        lget(f"w{dz}", "last", dyh=1, dz=dz)
    for gather in (a, b):
        for dyl in range(2):
            for dx in (0, -1, 1, 2):
                gather.sibling(dyl, dx)

    pairs = order // pair

    def depth(k):
        return pl.ds(pl.multiple_of(k * pair, 128), pair)

    def square_part(n):
        at_cols = slice(n * part, (n + 1) * part)
        square[:, at_cols] = jnp.dot(
            left[:, 0:pair], right[0, :, at_cols], preferred_element_type=jnp.float32
        )

        def step(k, carry):
            square[:, at_cols] += jnp.dot(
                left[:, depth(k)], right[k, :, at_cols], preferred_element_type=jnp.float32
            )
            return carry

        lax.fori_loop(1, pairs, step, 0)
        for i in range(rows // BLK):
            at_rows = slice(i * BLK, (i + 1) * BLK)
            for k in range(part // BLK):
                here = slice(k * BLK, (k + 1) * BLK)
                cols = slice(n * part + k * BLK, n * part + (k + 1) * BLK)
                scale = keep2[
                    row_id * (rows // BLK) + i, col_id * (width // BLK) + n * (part // BLK) + k
                ].astype(jnp.float32)
                kept = square[at_rows, cols] * scale
                square[at_rows, cols] = kept
                half[n, own, pl.ds(pl.multiple_of(core * rows + i * BLK, 16), BLK), here] = (
                    kept.astype(jnp.bfloat16)
                )

    fresh = set()
    stores = []

    def cube_dot(gather, n, dyl, dx):
        gather.sibling(dyl, dx)
        at_cols = slice(n * part, (n + 1) * part)
        k = (ylo + dyl) % 2 * XS + (x + dx + XS) % XS
        value = jnp.dot(left[:, depth(k)], half[n, k], preferred_element_type=jnp.float32)
        if n in fresh:
            o_ref[:, at_cols] += value
        else:
            o_ref[:, at_cols] = value
            fresh.add(n)

    def finish(n):
        for i in range(rows // BLK):
            at_rows = slice(i * BLK, (i + 1) * BLK)
            for k in range(part // BLK):
                cols = slice(n * part + k * BLK, n * part + (k + 1) * BLK)
                scale = keep3[
                    row_id * (rows // BLK) + i, col_id * (width // BLK) + n * (part // BLK) + k
                ].astype(jnp.float32)
                cube = o_ref[at_rows, cols] * scale
                o_ref[at_rows, cols] = 3.0 * square[at_rows, cols] - 2.0 * cube
        at_cols = slice(n * part, (n + 1) * part)
        store = pltpu.make_async_copy(o_ref.at[:, at_cols], out.at[:, at_cols], ls.at[4 + n])
        store.start()
        stores.append(store)

    a, b, c = [Gather(f"half{n}", half.at[n], n > 0) for n in range(cuts)]
    square_part(0)
    a.begin()
    square_part(1)
    b.begin()
    square_part(2)
    a.near(0)
    c.begin()
    b.turn()
    cube_dot(a, 0, 0, 0)
    a.far(0)
    a.across(0)
    b.near(0)
    cube_dot(b, 1, 0, 0)
    cube_dot(a, 0, 0, -1)
    c.turn()
    cube_dot(a, 0, 0, 1)
    cube_dot(a, 0, 1, 0)
    b.near(1)
    cube_dot(b, 1, 1, 0)
    a.across(-1)
    cube_dot(a, 0, 0, 2)
    cube_dot(b, 1, 0, -1)
    c.near(0)
    cube_dot(b, 1, 0, 1)
    cube_dot(c, 2, 0, 0)
    b.far(0)
    cube_dot(c, 2, 1, 0)
    cube_dot(a, 0, 1, -1)
    c.near(1)
    a.across(1)
    cube_dot(b, 1, 1, -1)
    cube_dot(b, 1, 1, 1)
    b.far(1)
    cube_dot(a, 0, 1, 1)
    cube_dot(b, 1, 0, 2)
    a.across(2)
    cube_dot(c, 2, 0, -1)
    cube_dot(c, 2, 0, 1)
    cube_dot(b, 1, 1, 2)
    finish(1)
    c.far(0)
    cube_dot(c, 2, 1, -1)
    cube_dot(c, 2, 1, 1)
    cube_dot(a, 0, 1, 2)
    finish(0)
    c.far(1)
    cube_dot(c, 2, 0, 2)
    cube_dot(c, 2, 1, 2)
    finish(2)
    for copy in started:
        copy.wait_send()
    for store in stores:
        store.wait()


def on_device(density, pattern, filter_square, filter_cube):
    rows_one, order = density.shape
    rows = order // lax.axis_size("row")
    width = order // lax.axis_size("col")
    cuts = 3
    pairs = order // (2 * rows)
    return pl.pallas_call(
        functools.partial(kernel, cuts),
        out_shape=jax.ShapeDtypeStruct((rows, width), jnp.float32),
        in_specs=[pl.BlockSpec(memory_space=pltpu.HBM)] * 4,
        out_specs=pl.BlockSpec(memory_space=pltpu.HBM),
        scratch_shapes=[
            pltpu.VMEM((rows_one, order), jnp.bfloat16),
            pltpu.VMEM((rows, width), jnp.float32),
            pltpu.VMEM((rows, order), jnp.bfloat16),
            pltpu.VMEM((pairs, 2 * rows, width), jnp.bfloat16),
            pltpu.VMEM((cuts, pairs, 2 * rows, width // cuts), jnp.bfloat16),
            pltpu.VMEM((rows, width), jnp.float32),
            pltpu.SMEM(pattern.shape, jnp.int32),
            pltpu.SMEM(pattern.shape, jnp.int32),
            pltpu.SMEM(pattern.shape, jnp.int32),
            pltpu.SemaphoreType.DMA((4 + cuts,)),
            pltpu.SemaphoreType.DMA((SEMS,)),
            pltpu.SemaphoreType.DMA((SEMS,)),
        ],
        compiler_params=pltpu.CompilerParams(
            collective_id=0, has_side_effects=True, vmem_limit_bytes=60 << 20
        ),
    )(density, pattern, filter_square, filter_cube)


def solution(mesh):
    placed = (P(("row", "col"), None), P(), P(), P())
    return jax.shard_map(
        on_device, mesh=mesh, in_specs=placed, out_specs=P("row", "col"), check_vma=False
    )
```

time: 114 us -> 99.9 us (0.88)
  Pallas kernels: 110 us -> 97.3 us
    pallas_call x1, Pallas kernels: 110 us -> 97.3 us  [on_device(): pl.pallas_call(functools.partial(kernel, cuts), out_shape=jax.ShapeDtypeS...]
    unnamed x11 -> x1, local copies, waits for them, and re-layouts: 2.35 us -> 2.36 us
where the time goes in v3:
time: 99.9 us; the launch traced here: 99.6 us
  Pallas kernels  97.3 us (97%)
  local copies, waits for them, and re-layouts  2.36 us (2%)
    pallas_call x1, Pallas kernels, on_device(): pl.pallas_call(functools.partial(kernel, cuts), out_shape=jax.ShapeDtypeS...  97.3 us
    unnamed x1, local copies, waits for them, and re-layouts  2.36 us

profile of v3, /device:TPU:1, one launch (start us, length us, event | category | flops | bytes accessed | tf_op | source)
XLA Modules:
  0.0 99.6 jit_solution(6174012341126613208)
XLA Ops:
  0.0 97.3 %shard_map.46 = f32[384,768]{1,0:T(8,128)} custom-call(bf16[48,6144]{1,0:T(8,128)(2,1)} %d_ref.1, s32[48,48]{1,0:T(8,128)} %p_ref.1, s32[48,48]{1,0:T(8,128)} %f2_ref.1, s32[48,48]{1,0:T(8,128)} %f3_ref.1), custom_call_target="tpu_custom_call" | custom-call | tf_op jit(solution)/shard_map/pallas_call | solution.py:385
  97.3 2.4 %copy.6 = f32[384,768]{1,0:T(8,128)} copy(f32[384,768]{1,0:T(8,128)} %shard_map.46) | data formatting | bytes 2359296

commit v4 on v3

--- a/solution.py
+++ b/solution.py
@@ -10,7 +10,7 @@
 BLK = 128
 XS, ZS = 4, 4
 MESH = pl.DeviceIdType.MESH
-SEMS = 128
+SEMS = 160
 
 
 def kernel(cuts, d_ref, p_ref, f2_ref, f3_ref, out, mine, o_ref, left, right, half, square, keep, keep2,
@@ -97,16 +97,17 @@
             ).astype(jnp.bfloat16)
     pl.semaphore_wait(barrier, len(partners))
 
-    def tile(buf, dyl=0, dx=0, dc=0, cut=None):
+    def tile(buf, dyl=0, dx=0, dc=0, cut=None, cols=slice(None)):
         c = (core + dc) % 2
         q = (ylo + dyl) % 2 * XS + (x + dx + XS) % XS
         number_of, of = cut or (0, 1)
         size = rows // of
-        return buf.at[q, pl.ds(pl.multiple_of(c * rows + number_of * size, 16), size), :]
+        return buf.at[q, pl.ds(pl.multiple_of(c * rows + number_of * size, 16), size), cols]
 
     class Gather:
-        def __init__(self, name, buf, y_first, halved=None):
+        def __init__(self, name, buf, y_first, halved=None, cols=slice(None)):
             self.name, self.buf, self.y_first, self.halved = name, buf, y_first, halved
+            self.cols = cols
 
         def view(self, part_of=None, **where):
             if self.halved is None:
@@ -115,7 +116,7 @@
                 cut = (self.halved, 2)
             else:
                 cut = (2 * self.halved + part_of, 4)
-            return tile(self.buf, cut=cut, **where)
+            return tile(self.buf, cut=cut, cols=self.cols, **where)
 
         def put(self, what, target, **where):
             ref = self.view(**where)
@@ -124,9 +125,10 @@
         def get(self, what, **where):
             receive((self.name, what), self.view(**where))
 
-        def begin(self):
-            self.put("x+0", at(dx=1))
-            self.put("x-0", at(dx=-1))
+        def begin(self, whole=True):
+            if whole:
+                self.put("x+0", at(dx=1))
+                self.put("x-0", at(dx=-1))
             self.put("y0", at(dyl=1))
             self.put("c00", at(dc=1))
 
@@ -136,10 +138,12 @@
             self.put("x-1", at(dx=-1), dyl=1)
             self.put("c10", at(dc=1), dyl=1)
 
-        def near(self, dyl):
-            self.get(f"x+{dyl}", dyl=dyl, dx=-1)
+        def near(self, dyl, whole=True):
+            if whole:
+                self.get(f"x+{dyl}", dyl=dyl, dx=-1)
             self.put(f"f+{dyl}", at(dx=1), dyl=dyl, dx=-1, part_of=0)
-            self.get(f"x-{dyl}", dyl=dyl, dx=1)
+            if whole:
+                self.get(f"x-{dyl}", dyl=dyl, dx=1)
             self.put(f"f-{dyl}", at(dx=-1), dyl=dyl, dx=1, part_of=1)
             for dx in (-1, 1):
                 if not self.y_first:
@@ -161,7 +165,8 @@
             self.get(f"c{dyl}{dx}", dyl=dyl, dx=dx, dc=1)
 
     spans = {
-        "most": (lambda h: (1 - h) * (order // 4), 3 * order // 4),
+        "one": (lambda h: (1 - h) * (order // 4), 3 * order // 8),
+        "two": (lambda h: (1 - h) * (order // 4) + 3 * order // 8, 3 * order // 8),
         "far": (lambda h: (1 - h) * (order // 2), order // 2),
         "mid": (lambda h: (1 + h) * (order // 4), order // 4),
         "last": (lambda h: h * (3 * order // 4), order // 4),
@@ -198,9 +203,9 @@
 
     own = ylo * XS + x
 
-    def own_rows(source):
+    def own_rows(source, dx=0):
         start = pl.multiple_of(core * rows + source * rows_one, 16)
-        return right.at[own, pl.ds(start, rows_one), :]
+        return right.at[ylo * XS + (x + dx + XS) % XS, pl.ds(start, rows_one), :]
 
     def grid_begin(dyh):
         source = at(dyh=dyh)[1]
@@ -210,55 +215,22 @@
             send(("grid", dyh, dz), block, own_rows(source), device)
         own_rows(source)[...] = left[piece(source), columns(col_id)]
 
-    def grid_end(dyh):
-        for dz in (1, 3, 2):
-            receive(("grid", dyh, dz), own_rows(at(dyh=dyh, dz=-dz)[1]))
-
-    a = Gather("right0", right, True, yhi)
-    b = Gather("right1", right, True, (yhi + 1) % 2)
-    grid_begin(0)
-    lput("q", "far", at(dyh=1))
-    settle(3)
-    lbegin("last", 0)
-    grid_end(0)
-    a.begin()
-    lget("q", "far", dyh=1)
-    grid_begin(1)
-    lput("q", "mid", at(dyh=1))
-    lbegin("most", 0)
-    lbegin("far", 1)
-    lnear("last", 0)
-    a.near(0)
-    a.turn()
-    grid_end(1)
-    b.begin()
-    lget("q", "mid", dyh=1)
-    lbegin("mid", 1)
-    a.far(0)
-    a.near(1)
-    b.turn()
-    b.near(0)
-    for dz in (0, 1, -1):
-        lput(f"w{dz}", "last", at(dyh=1), dz=dz)
-    lnear("most", 0)
-    lfar("last", 0)
-    lput("w2", "last", at(dyh=1), dz=2)
-    lnear("far", 1)
-    lnear("mid", 1)
-    a.far(1)
-    b.near(1)
-    b.far(0)
-    b.far(1)
-    lfar("most", 0)
-    lfar("far", 1)
-    lfar("mid", 1)
-    for dz in (0, 1, -1, 2):
-        lget(f"w{dz}", "last", dyh=1, dz=dz)
-    for gather in (a, b):
-        for dyl in range(2):
-            for dx in (0, -1, 1, 2):
-                gather.sibling(dyl, dx)
-
+    def grid_end(dyh, dz):
+        receive(("grid", dyh, dz), own_rows(at(dyh=dyh, dz=-dz)[1]))
+
+    def feed(dz):
+        block = own_rows(at(dz=-dz)[1])
+        send(("feed+", dz), block, block, at(dx=1))
+        send(("feed-", dz), block, block, at(dx=-1))
+
+    def fed(dz):
+        source = at(dz=-dz)[1]
+        receive(("feed+", dz), own_rows(source, -1))
+        receive(("feed-", dz), own_rows(source, 1))
+
+    ga = Gather("right0", right, True, yhi)
+    g0 = Gather("right1", right, True, (yhi + 1) % 2, slice(0, part))
+    g1 = Gather("right2", right, True, (yhi + 1) % 2, slice(part, width))
     pairs = order // pair
 
     def depth(k):
@@ -266,17 +238,24 @@
 
     def square_part(n):
         at_cols = slice(n * part, (n + 1) * part)
-        square[:, at_cols] = jnp.dot(
-            left[:, 0:pair], right[0, :, at_cols], preferred_element_type=jnp.float32
-        )
-
         def step(k, carry):
-            square[:, at_cols] += jnp.dot(
-                left[:, depth(k)], right[k, :, at_cols], preferred_element_type=jnp.float32
+            value = jnp.dot(
+                left[:, pl.ds(pl.multiple_of(k * 2 * pair, 128), 2 * pair)],
+                right[pl.ds(2 * k, 2), :, at_cols].reshape(2 * pair, part),
+                preferred_element_type=jnp.float32,
             )
+
+            @pl.when(k == 0)
+            def _():
+                square[:, at_cols] = value
+
+            @pl.when(k > 0)
+            def _():
+                square[:, at_cols] += value
+
             return carry
 
-        lax.fori_loop(1, pairs, step, 0)
+        lax.fori_loop(0, pairs // 2, step, 0)
         for i in range(rows // BLK):
             at_rows = slice(i * BLK, (i + 1) * BLK)
             for k in range(part // BLK):
@@ -320,9 +299,69 @@
         store.start()
         stores.append(store)
 
+    grid_begin(0)
+    feed(0)
+    lput("q", "far", at(dyh=1))
+    settle(3)
+    lbegin("last", 0)
+    lbegin("one", 0)
+    for dz in (1, 3, 2):
+        grid_end(0, dz)
+        feed(dz)
+    ga.begin(False)
+    lget("q", "far", dyh=1)
+    grid_begin(1)
+    lput("q", "mid", at(dyh=1))
+    lbegin("two", 0)
+    lbegin("far", 1)
+    lnear("last", 0)
+    for dz in range(ZS):
+        fed(dz)
+    ga.near(0, False)
+    ga.turn()
+    for dz in (1, 3, 2):
+        grid_end(1, dz)
+    g0.begin()
+    lget("q", "mid", dyh=1)
+    lbegin("mid", 1)
+    ga.far(0)
+    g1.begin()
+    lnear("one", 0)
+    ga.near(1)
+    g0.turn()
+    g0.near(0)
+    for dz in (0, 1, -1):
+        lput(f"w{dz}", "last", at(dyh=1), dz=dz)
+    lfar("last", 0)
+    lput("w2", "last", at(dyh=1), dz=2)
+    lnear("two", 0)
+    g1.turn()
+    g0.near(1)
+    lnear("far", 1)
+    lnear("mid", 1)
+    g1.near(0)
+    ga.far(1)
+    g0.far(0)
+    g0.far(1)
+    g1.near(1)
+    lfar("one", 0)
+    lfar("two", 0)
+    lfar("far", 1)
+    lfar("mid", 1)
+    for dz in (0, 1, -1, 2):
+        lget(f"w{dz}", "last", dyh=1, dz=dz)
+    for gather in (ga, g0):
+        for dyl in range(2):
+            for dx in (0, -1, 1, 2):
+                gather.sibling(dyl, dx)
     a, b, c = [Gather(f"half{n}", half.at[n], n > 0) for n in range(cuts)]
     square_part(0)
     a.begin()
+    g1.far(0)
+    g1.far(1)
+    for dyl in range(2):
+        for dx in (0, -1, 1, 2):
+            g1.sibling(dyl, dx)
     square_part(1)
     b.begin()
     square_part(2)
@@ -370,6 +409,7 @@
     cube_dot(c, 2, 0, 2)
     cube_dot(c, 2, 1, 2)
     finish(2)
+    assert len(names) <= SEMS
     for copy in started:
         copy.wait_send()
     for store in stores:

time: 99.9 us -> 95.7 us (0.958)
  Pallas kernels: 97.3 us -> 93.1 us
    pallas_call x1, Pallas kernels: 97.3 us -> 93.1 us  [on_device(): pl.pallas_call(functools.partial(kernel, cuts), out_shape=jax.ShapeDtypeS...]
where the time goes in v4:
time: 95.7 us; the launch traced here: 95.5 us
  Pallas kernels  93.1 us (97%)
  local copies, waits for them, and re-layouts  2.36 us (2%)
    pallas_call x1, Pallas kernels, on_device(): pl.pallas_call(functools.partial(kernel, cuts), out_shape=jax.ShapeDtypeS...  93.1 us
    unnamed x1, local copies, waits for them, and re-layouts  2.36 us

profile of v4, /device:TPU:1, one launch (start us, length us, event | category | flops | bytes accessed | tf_op | source)
XLA Modules:
  0.0 95.5 jit_solution(8087776088630123492)
XLA Ops:
  0.0 93.1 %shard_map.46 = f32[384,768]{1,0:T(8,128)} custom-call(bf16[48,6144]{1,0:T(8,128)(2,1)} %d_ref.1, s32[48,48]{1,0:T(8,128)} %p_ref.1, s32[48,48]{1,0:T(8,128)} %f2_ref.1, s32[48,48]{1,0:T(8,128)} %f3_ref.1), custom_call_target="tpu_custom_call" | custom-call | tf_op jit(solution)/shard_map/pallas_call | solution.py:425
  93.2 2.4 %copy.6 = f32[384,768]{1,0:T(8,128)} copy(f32[384,768]{1,0:T(8,128)} %shard_map.46) | data formatting | bytes 2359296

commit v5 on v4

--- a/solution.py
+++ b/solution.py
@@ -146,9 +146,11 @@
                 self.get(f"x-{dyl}", dyl=dyl, dx=1)
             self.put(f"f-{dyl}", at(dx=-1), dyl=dyl, dx=1, part_of=1)
             for dx in (-1, 1):
-                if not self.y_first:
-                    self.put(f"y{dx}", at(dyl=1), dx=dx)
                 self.put(f"c{dyl}{dx}", at(dc=1), dyl=dyl, dx=dx)
+
+        def over(self):
+            for dx in (-1, 1):
+                self.put(f"y{dx}", at(dyl=1), dx=dx)
 
         def far(self, dyl):
             self.get(f"f+{dyl}", dyl=dyl, dx=-2, part_of=0)
@@ -322,23 +324,23 @@
     for dz in (1, 3, 2):
         grid_end(1, dz)
     g0.begin()
+    lnear("one", 0)
     lget("q", "mid", dyh=1)
     lbegin("mid", 1)
     ga.far(0)
     g1.begin()
-    lnear("one", 0)
     ga.near(1)
+    lnear("two", 0)
     g0.turn()
     g0.near(0)
+    lnear("far", 1)
     for dz in (0, 1, -1):
         lput(f"w{dz}", "last", at(dyh=1), dz=dz)
     lfar("last", 0)
     lput("w2", "last", at(dyh=1), dz=2)
-    lnear("two", 0)
     g1.turn()
+    lnear("mid", 1)
     g0.near(1)
-    lnear("far", 1)
-    lnear("mid", 1)
     g1.near(0)
     ga.far(1)
     g0.far(0)
@@ -367,6 +369,7 @@
     square_part(2)
     a.near(0)
     c.begin()
+    a.over()
     b.turn()
     cube_dot(a, 0, 0, 0)
     a.far(0)

time: 95.7 us -> 94 us (0.982)
  Pallas kernels: 93.1 us -> 91.4 us
    pallas_call x1, Pallas kernels: 93.1 us -> 91.4 us  [on_device(): pl.pallas_call(functools.partial(kernel, cuts), out_shape=jax.ShapeDtypeS...]
where the time goes in v5:
time: 94 us; the launch traced here: 93.8 us
  Pallas kernels  91.4 us (97%)
  local copies, waits for them, and re-layouts  2.36 us (3%)
    pallas_call x1, Pallas kernels, on_device(): pl.pallas_call(functools.partial(kernel, cuts), out_shape=jax.ShapeDtypeS...  91.4 us
    unnamed x1, local copies, waits for them, and re-layouts  2.36 us

profile of v5, /device:TPU:1, one launch (start us, length us, event | category | flops | bytes accessed | tf_op | source)
XLA Modules:
  0.0 93.8 jit_solution(3612448479907472717)
XLA Ops:
  0.0 91.4 %shard_map.46 = f32[384,768]{1,0:T(8,128)} custom-call(bf16[48,6144]{1,0:T(8,128)(2,1)} %d_ref.1, s32[48,48]{1,0:T(8,128)} %p_ref.1, s32[48,48]{1,0:T(8,128)} %f2_ref.1, s32[48,48]{1,0:T(8,128)} %f3_ref.1), custom_call_target="tpu_custom_call" | custom-call | tf_op jit(solution)/shard_map/pallas_call | solution.py:428
  91.4 2.4 %copy.6 = f32[384,768]{1,0:T(8,128)} copy(f32[384,768]{1,0:T(8,128)} %shard_map.46) | data formatting | bytes 2359296
